TPU v7x, 32 devices: a whole 2x2x4 slice. The times are simulated.
32 devices in a mesh: groups: 2 (over x), expert: 16 (over z, y, core).
Axes of the slice: x: 2, y: 2, z: 4, core: 2. Of those that a mesh axis runs over, the one named last changes fastest.
Arguments:
- hidden_in: bfloat16 [256, 4096], P(('groups', 'expert')), parts along dimension 0, may hold values from -6 to 6
- queries: bfloat16 [256, 4096], P(('groups', 'expert')), parts along dimension 0, may hold values from -8 to 8
- decode_key_value: bfloat16 [256, 2, 256], P(('groups', 'expert')), parts along dimension 0, may hold values from -6 to 6
- local_kv: bfloat16 [1024, 2, 16, 256], P(('groups', 'expert')), parts along dimension 0, may hold values from -8 to 8
- page_table: int32 [256, 16], P(('groups', 'expert')), parts along dimension 0, may hold values from 0 to 31
- seq_blocks: int32 [256], P(('groups', 'expert')), parts along dimension 0, may hold values from 1 to 16
- prompt_kv: bfloat16 [32, 16, 2, 16, 256], P(('groups', 'expert')), parts along dimension 0, may hold values from -8 to 8
- prompt_owner: int32 [32], P('groups'), parts along dimension 0, may hold values from 0 to 15, as said below
- prompt_pages: int32 [32], P('groups'), parts along dimension 0, may hold values from 1 to 16
- norm_gain: float32 [4096], replicated, may hold values from 0.5 to 1.5
- router: bfloat16 [4096, 8], replicated, may hold values from -0.09375 to 0.09375
- w_gate: bfloat16 [16, 4096, 384], P('expert'), may hold values from -0.09375 to 0.09375
- w_up: bfloat16 [16, 4096, 384], P('expert'), may hold values from -0.09375 to 0.09375
- w_down: bfloat16 [16, 384, 4096], P('expert'), may hold values from -0.21875 to 0.21875
- route_ids: int32 [256, 8], P(('groups', 'expert')), parts along dimension 0, may hold values from 0 to 7, as said below
Outputs:
- layer_out: bfloat16 [256, 4096], P(('groups', 'expert')), parts along dimension 0
There are 2 independent parts, one for each index of `groups`. A program takes and returns all parts, laid end to end along the dimension named above; an argument that names none is the same for every part. Nothing has to cross between parts.
Inputs may be any that keep to these rules, and one draw needn't show every extreme that they name: `prompt_owner`: each device is named by at most 2 prompts, and by exactly 2 for some of the devices. `route_ids`: each row names 8 different experts; among the rows of one device no expert is named more than 8 times, a bound that some block reaches. `page_table`: indices among the pages of the sequence's own device.
All inputs are finite; a program needn't handle non-finite values.
Results may differ from a plain program's by a relative error of at most 0.0056.
Values may be sent and summed in bfloat16 or wider, within the bound.
No kernel may reach another device: no remote copies, remote signals or barrier semaphores. Data moves between devices by JAX's collectives and lax.ppermute only.
A program may use at most 128 MiB of HBM per device.

v0:
```python
import math
import jax
import jax.numpy as jnp
from jax import lax
from jax.sharding import PartitionSpec as P

D = 4096
QUERY_HEADS = 32
KEY_VALUE_HEADS = 2
HEAD_SIZE = 128
PAGE_TOKENS = 16
TOPK = 8
MAXB = 16
MAXP = 2
norm_eps = 1e-06
masked_score = -1e30


def partner(x, axis, apart):
    return lax.ppermute(x, axis, [(i, i ^ 1 << apart) for i in range(lax.axis_size(axis))])


def attend(rows_of_queries, rows_of_keys, rows_of_values, allowed, token_own_key, token_own_value):
    decode_tokens = rows_of_queries.shape[0]
    heads_of_queries = rows_of_queries.reshape(
        decode_tokens, KEY_VALUE_HEADS, QUERY_HEADS // KEY_VALUE_HEADS, HEAD_SIZE
    )
    heads_of_keys = rows_of_keys.reshape(decode_tokens, -1, KEY_VALUE_HEADS, HEAD_SIZE)
    heads_of_values = rows_of_values.reshape(decode_tokens, -1, KEY_VALUE_HEADS, HEAD_SIZE)
    scale_for_scores = 1.0 / math.sqrt(HEAD_SIZE)
    allowed_mask = allowed[:, None, None, :]
    scores = (
        jnp.einsum(
            "tkgd,tlkd->tkgl", heads_of_queries, heads_of_keys, preferred_element_type=jnp.float32
        )
        * scale_for_scores
    )
    scores = jnp.where(allowed_mask, scores, masked_score)
    token_own_score = (
        jnp.einsum(
            "xejp,xep->xej",
            heads_of_queries,
            token_own_key.reshape(decode_tokens, KEY_VALUE_HEADS, HEAD_SIZE),
            preferred_element_type=jnp.float32,
        )
        * scale_for_scores
    )
    peak = jnp.maximum(jnp.max(scores, -1), token_own_score)
    weights = jnp.where(allowed_mask, jnp.exp(scores - peak[..., None]), 0.0)
    own_weight = jnp.exp(token_own_score - peak)
    denominator = jnp.sum(weights, -1) + own_weight
    probs = (weights / denominator[..., None]).astype(jnp.bfloat16)
    token_own_probability = (own_weight / denominator).astype(jnp.bfloat16)
    blended_noise = jnp.einsum(
        "tkgl,tlkd->tkgd", probs, heads_of_values, preferred_element_type=jnp.float32
    )
    blended_noise = blended_noise + token_own_probability.astype(jnp.float32)[
        ..., None
    ] * token_own_value.reshape(decode_tokens, KEY_VALUE_HEADS, 1, HEAD_SIZE).astype(jnp.float32)
    return blended_noise.reshape(decode_tokens, QUERY_HEADS * HEAD_SIZE).astype(jnp.bfloat16)


def all_tokens(resid_wide, normed, spread, w_gate, w_up, w_down):
    devices = lax.axis_size("expert")
    seq_dev, experts = spread.shape
    expert = lax.axis_index("expert") // 2
    bits = devices.bit_length() - 1
    coarse = lax.reduce_precision(spread, 8, 7)
    fine = spread - coarse
    pad = -2 * experts % 128
    tail = jnp.pad(jnp.concatenate([coarse, fine], 1), ((0, 0), (0, pad))).astype(jnp.bfloat16)
    rows = jnp.concatenate([normed, tail], 1)
    for bit in reversed(range(bits)):
        rows = jnp.concatenate([rows, partner(rows, "expert", bit)], 0)
    gates = rows[:, D : D + 2 * experts].astype(jnp.float32).reshape(-1, 2, experts)
    own = jnp.arange(experts, dtype=jnp.int32) == expert
    gate = jnp.sum(jnp.where(own, gates, 0.0), (1, 2))
    tokens = rows[:, :D]
    gate_proj = jnp.dot(tokens, w_gate, preferred_element_type=jnp.float32)
    up_proj = jnp.dot(tokens, w_up, preferred_element_type=jnp.float32)
    activated = (jax.nn.silu(gate_proj) * up_proj).astype(jnp.bfloat16)
    mixed = jnp.dot(activated, w_down, preferred_element_type=jnp.float32) * gate[:, None]
    for bit in range(bits):
        half = mixed.shape[0] // 2
        moved = partner(mixed[half:].astype(jnp.bfloat16), "expert", bit)
        mixed = mixed[:half] + moved.astype(jnp.float32)
    return (resid_wide + mixed).astype(jnp.bfloat16)


def local(
    hidden_in,
    queries,
    decode_key_value,
    local_kv,
    page_table,
    seq_blocks,
    prompt_kv,
    prompt_owner,
    prompt_pages,
    norm_gain,
    router,
    w_gate,
    w_up,
    w_down,
    route_ids,
):
    devices = lax.axis_size("expert")
    position = lax.axis_index("expert")
    experts = devices // 2
    seq_dev = hidden_in.shape[0]
    key_value_width = KEY_VALUE_HEADS * HEAD_SIZE
    capacity = min(seq_dev, max(2, 2 * ((3 * seq_dev * TOPK + 2 * devices - 1) // (2 * devices))))
    half_cap = capacity // 2
    even_core = position % 2 == 0
    prompt_count = prompt_owner.shape[0]
    prompt_range = jnp.arange(prompt_count, dtype=jnp.int32)
    same_owner = prompt_owner[:, None] == prompt_owner[None, :]
    earlier = prompt_range[None, :] < prompt_range[:, None]
    arrival = jnp.sum((same_owner & earlier).astype(jnp.int32), 1)
    matching = (
        prompt_owner[None, None, :] == jnp.arange(devices, dtype=jnp.int32)[:, None, None]
    ) & (arrival[None, None, :] == jnp.arange(MAXP, dtype=jnp.int32)[None, :, None])
    chosen_prompt = jnp.sum(jnp.where(matching, prompt_range[None, None, :], 0), -1)
    occupied = jnp.any(matching, -1)
    own_picks = lax.dynamic_index_in_dim(chosen_prompt, position, 0, keepdims=False)
    own_occupied = lax.dynamic_index_in_dim(occupied, position, 0, keepdims=False)
    page_rows = prompt_kv[0]
    outgoing = jnp.take(page_rows, chosen_prompt.T.reshape(-1), axis=0).reshape(
        MAXP, devices, 2, PAGE_TOKENS, key_value_width
    )
    outgoing = jnp.where(occupied.T[:, :, None, None, None], outgoing, 0)
    arrived = lax.all_to_all(outgoing, "expert", split_axis=1, concat_axis=1, tiled=True)
    lengths = jnp.take(prompt_pages, own_picks)
    new_keys = arrived[:, :, 0].reshape(MAXP, devices * PAGE_TOKENS, key_value_width)
    new_values = arrived[:, :, 1].reshape(MAXP, devices * PAGE_TOKENS, key_value_width)
    new_allowed = (jnp.arange(devices * PAGE_TOKENS, dtype=jnp.int32) // PAGE_TOKENS)[
        None, :
    ] < lengths[:, None]
    fresh_rows = attend(
        queries[:MAXP],
        new_keys,
        new_values,
        new_allowed,
        decode_key_value[:MAXP, 0],
        decode_key_value[:MAXP, 1],
    )
    fetched = local_kv[page_table]
    old_keys = fetched[:, :, 0].reshape(seq_dev, MAXB * PAGE_TOKENS, key_value_width)
    old_values = fetched[:, :, 1].reshape(seq_dev, MAXB * PAGE_TOKENS, key_value_width)
    old_allowed = (jnp.arange(MAXB * PAGE_TOKENS, dtype=jnp.int32) // PAGE_TOKENS)[
        None, :
    ] < seq_blocks[:, None]
    old_out = attend(
        queries, old_keys, old_values, old_allowed, decode_key_value[:, 0], decode_key_value[:, 1]
    )
    new_count = jnp.sum(own_occupied.astype(jnp.int32))
    is_new = jnp.arange(MAXP, dtype=jnp.int32) < new_count
    attention = jnp.concatenate(
        [jnp.where(is_new[:, None], fresh_rows, old_out[:MAXP]), old_out[MAXP:]], 0
    )
    residual = (hidden_in.astype(jnp.float32) + attention.astype(jnp.float32)).astype(jnp.bfloat16)
    resid_wide = residual.astype(jnp.float32)
    normed = (
        resid_wide
        * lax.rsqrt(jnp.mean(resid_wide * resid_wide, -1, keepdims=True) + norm_eps)
        * norm_gain
    ).astype(jnp.bfloat16)
    logits = jnp.dot(normed, router, preferred_element_type=jnp.float32)
    expert_onehot = route_ids[:, :, None] == jnp.arange(experts, dtype=jnp.int32)[None, None, :]
    selected = jnp.sum(jnp.where(expert_onehot, logits[:, None, :], 0.0), -1)
    gate_weights = jax.nn.softmax(selected, -1)
    if capacity >= seq_dev and devices & devices - 1 == 0:
        spread = jnp.sum(jnp.where(expert_onehot, gate_weights[:, :, None], 0.0), 1)
        return all_tokens(resid_wide, normed, spread, w_gate[0], w_up[0], w_down[0])
    assigned = seq_dev * TOPK
    expert_ids = route_ids.reshape(assigned)
    chosen = (expert_ids[:, None] == jnp.arange(experts, dtype=jnp.int32)[None, :]).astype(
        jnp.int32
    )
    before = jnp.cumsum(chosen, 0) - chosen
    slot_rank = jnp.sum(before * chosen, 1)
    slot_index = expert_ids * capacity + slot_rank
    placing = slot_index[None, :] == jnp.arange(experts * capacity, dtype=jnp.int32)[:, None]
    selector = jnp.any(placing.reshape(experts * capacity, seq_dev, TOPK), -1).astype(jnp.bfloat16)
    gathered_rows = jnp.dot(selector, normed, preferred_element_type=jnp.float32).astype(
        jnp.bfloat16
    )
    outgoing_half = gathered_rows.reshape(devices, half_cap, D)
    own_half = lax.all_to_all(outgoing_half, "expert", split_axis=0, concat_axis=0, tiled=True)
    partner_half = partner(own_half, "expert", 0)
    received = jnp.where(
        even_core,
        jnp.concatenate([own_half, partner_half], 1),
        jnp.concatenate([partner_half, own_half], 1),
    )
    flattened = received.reshape(devices * capacity, D)
    gate_proj = jnp.dot(flattened, w_gate[0], preferred_element_type=jnp.float32)
    up_proj = jnp.dot(flattened, w_up[0], preferred_element_type=jnp.float32)
    activated = (jax.nn.silu(gate_proj) * up_proj).astype(jnp.bfloat16)
    partial_value = jnp.dot(activated, w_down[0], preferred_element_type=jnp.float32).reshape(
        devices, capacity, D
    )
    kept = jnp.where(even_core, partial_value[:, :half_cap], partial_value[:, half_cap:])
    handed = jnp.where(even_core, partial_value[:, half_cap:], partial_value[:, :half_cap])
    partner_part = partner(handed, "expert", 0)
    finished = (kept + partner_part).astype(jnp.bfloat16)
    returned = lax.all_to_all(finished, "expert", split_axis=0, concat_axis=0, tiled=True)
    expert_sum = returned.reshape(experts * capacity, D)
    picked = jnp.take(expert_sum, slot_index, axis=0).astype(jnp.float32).reshape(seq_dev, TOPK, D)
    expert_mix = jnp.sum(picked * gate_weights[:, :, None], 1)
    return (resid_wide + expert_mix).astype(jnp.bfloat16)


def solution(mesh):
    return jax.shard_map(
        local,
        mesh=mesh,
        in_specs=(
            P(("groups", "expert"), None),
            P(("groups", "expert"), None),
            P(("groups", "expert"), None, None),
            P(("groups", "expert"), None, None, None),
            P(("groups", "expert"), None),
            P(("groups", "expert")),
            P(("groups", "expert"), None, None, None, None),
            P("groups"),
            P("groups"),
            P(),
            P(),
            P("expert", None, None),
            P("expert", None, None),
            P("expert", None, None),
            P(("groups", "expert"), None),
        ),
        out_specs=P(("groups", "expert"), None),
        check_vma=False,
    )
```

profile of v0, /device:TPU:0, one launch (start us, length us, event | category | flops | bytes accessed | tf_op | source)
XLA Modules:
  0.0 98.2 jit_solution(18162269884148207099)
XLA Ops:
  0.0 1.0 %convert_reduce_fusion = s32[16]{0:T(128)S(1)} fusion(s32[16]{0:T(128)} %param.22), kind=kLoop, calls=%fused_computation.86 | loop fusion | flops 1264 | bytes 128 | tf_op jit(solution)/shard_map/reduce_sum | solution.py:119
  1.0 0.7 iota_compare_fusion.2
  1.7 0.1 fusion.43
  1.8 0.1 and_reduce_fusion
  1.9 0.7 compare_select_fusion
  2.8 2.3 %gather_fusion.1 = bf16[32,2,16,256]{3,2,1,0:T(8,128)(2,1)} fusion(bf16[16,2,16,256]{3,2,1,0:T(8,128)(2,1)} %bitcast.87, s32[1024]{0:T(1024)S(1)} %get-tuple-element.26), kind=kCustom, calls=%fused_computation.1 | custom fusion | bytes 1048704 | tf_op jit(solution)/shard_map/jit(_take)/gather | solution.py:128
  5.1 1.2 %select_select_fusion = bf16[2,16,2,16,256]{4,3,2,1,0:T(8,128)(2,1)S(1)} fusion(bf16[2,16,2,16,256]{4,3,2,1,0:T(8,128)(2,1)} %bitcast.86, pred[2,16]{1,0:T(4,128)(4,1)S(1)} %compare_and_fusion, pred[2,16]{1,0:T(4,128)(4,1)S(1)} %bitcast.99), kind=kLoop, calls=%fused_computation.30 | loop fusion | flops 524288 | bytes 1048640 | tf_op jit(solution)/shard_map/jit(_where)/select_n | solution.py:131
  6.3 0.9 copy.48
  7.2 7.5 %all-to-all-start = ((bf16[2,16,2,16,256]{4,3,0,2,1:T(8,128)(2,1)}), bf16[2,16,2,16,256]{4,3,0,2,1:T(8,128)(2,1)}, u32[]{:S(2)}, u32[]{:S(2)}) async-start(bf16[2,16,2,16,256]{4,3,0,2,1:T(8,128)(2,1)} %copy.48), calls=%async_computation | async-start | bytes 1048576 | tf_op jit(solution)/shard_map/all_to_all | solution.py:132
  14.7 3.1 %gather_fusion.2 = bf16[128,2,16,256]{3,2,1,0:T(8,128)(2,1)} fusion(bf16[32,2,16,256]{3,2,1,0:T(8,128)(2,1)} %param.18, s32[1024]{0:T(1024)S(1)} %get-tuple-element.25), kind=kCustom, calls=%fused_computation.2 | custom fusion | bytes 4194816 | tf_op jit(solution)/shard_map/gather | solution.py:147
  17.8 3.0 %slice_bitcast_fusion.1 = (bf16[8,16,1,16,256]{4,3,1,0,2:T(8,128)(2,1)}, bf16[8,16,1,16,256]{4,3,1,0,2:T(8,128)(2,1)}) fusion(bf16[8,16,2,16,256]{4,3,2,1,0:T(8,128)(2,1)} %bitcast.85), kind=kLoop, calls=%fused_computation.22 | loop fusion | bytes 4194304
  20.8 2.2 %reshape_reshape_squeeze.15 = bf16[8,256,2,128]{3,2,1,0:T(2,128)(2,1)} reshape(bf16[8,16,1,16,256]{4,3,1,0,2:T(8,128)(2,1)} %get-tuple-element.8) | data formatting | bytes 2097152 | tf_op jit(solution)/shard_map/reshape;reshape;squeeze | solution.py:29
  23.0 2.2 %reshape_reshape_squeeze.14 = bf16[8,256,2,128]{3,2,1,0:T(2,128)(2,1)} reshape(bf16[8,16,1,16,256]{4,3,1,0,2:T(8,128)(2,1)} %get-tuple-element.7) | data formatting | bytes 2097152 | tf_op jit(solution)/shard_map/reshape;reshape;squeeze | solution.py:28
  25.3 0.1 fusion.35
  25.5 1.8 %fusion.66 = (f32[8,2,16]{2,1,0:T(2,128)S(1)}, f32[8,2,16,256]{3,2,1,0:T(8,128)S(1)}) fusion(bf16[8,2,16,128]{3,0,2,1:T(8,128)(2,1)S(1)} %bitcast.103, bf16[8,256,2,128]{3,2,1,0:T(2,128)(2,1)} %reshape_reshape_squeeze.14, pred[8,256]{1,0:T(8,128)(4,1)S(1)} %broadcast_compare_fusion), kind=kOutput, calls=%fused_computation.142 | convolution fusion | flops 16973568 | bytes 1379328 | tf_op jit(solution)/shard_map/tkgd,tlkd->tkgl/dot_general | solution.py:33
  27.3 0.2 fusion.17
  27.6 0.3 fusion.7
  28.0 0.7 fusion.56
  28.7 0.6 gather_fusion
  29.4 1.1 %iota_compare_fusion.6 = pred[2]{0:T(512)(128)(4,1)} fusion(s32[]{:T(128)} %get-tuple-element.27), kind=kLoop, calls=%fused_computation.135 | loop fusion | flops 2 | bytes 6 | tf_op jit(solution)/shard_map/lt | solution.py:157
  30.4 0.6 broadcast_compare_fusion.1
  31.1 0.6 slice_convert_fusion.5
  31.7 0.7 fusion.53
  32.4 1.8 %fusion.65 = (bf16[2,16,1,16,256]{4,3,0,2,1:T(8,128)(2,1)}, bf16[2,16,1,16,256]{4,3,0,2,1:T(8,128)(2,1)S(1)}) fusion(bf16[2,16,2,16,256]{4,3,0,2,1:T(8,128)(2,1)} %all-to-all-done), kind=kLoop, calls=%fused_computation.141 | loop fusion | bytes 1048576 | tf_op jit(solution)/shard_map/slice | solution.py:134
  34.2 0.8 reshape_reshape_squeeze.13
  34.9 1.0 %copy.49 = bf16[2,16,1,16,256]{4,3,1,0,2:T(8,128)(2,1)S(1)} copy(bf16[2,16,1,16,256]{4,3,0,2,1:T(8,128)(2,1)} %get-tuple-element.9) | data formatting | bytes 524288 | tf_op jit(solution)/shard_map/slice | solution.py:134
  35.9 0.8 reshape_reshape_squeeze.12
  36.7 1.3 %fusion.67 = (f32[2,2,16]{2,1,0:T(2,128)S(1)}, f32[2,2,16,256]{3,2,1,0:T(8,128)S(1)}) fusion(bf16[2,2,16,128]{3,2,1,0:T(8,128)(2,1)} %bitcast.95, bf16[2,256,2,128]{3,2,1,0:T(2,128)(2,1)} %reshape_reshape_squeeze.12, pred[2,256]{1,0:T(4,128)(4,1)} %broadcast_compare_fusion.1), kind=kOutput, calls=%fused_computation.143 | convolution fusion | flops 4243392 | bytes 344832 | tf_op jit(solution)/shard_map/tkgd,tlkd->tkgl/dot_general | solution.py:33
  38.0 0.7 multiply_maximum_fusion.1
  38.6 0.8 fusion.38
  39.4 0.7 fusion.57
  40.1 1.2 %fusion.10 = bf16[2,2,16,128]{3,2,1,0:T(8,128)(2,1)S(1)} fusion(bf16[2,256,2,128]{3,2,1,0:T(2,128)(2,1)} %reshape_reshape_squeeze.13, f32[2,2,16,256]{3,2,1,0:T(8,128)S(1)} %get-tuple-element.24, f32[2,2,16]{2,1,0:T(2,128)S(1)} %get-tuple-element.18, f32[2,2,16]{2,1,0:T(2,128)S(1)} %multiply_maximum_fusion.1, pred[2,256]{1,0:T(4,128)(4,1)} %broadcast_compare_fusion.1, ...), kind=kOutput, calls=%fused_computation.18 | convolution fusion | flops 4284416 | bytes 347392 | tf_op jit(solution)/shard_map/tkgl,tlkd->tkgd/dot_general | solution.py:54
  41.4 0.2 fusion.18
  41.7 0.1 fusion.68
  41.8 0.2 select_reduce_fusion.2
  42.0 0.1 reduce_max.29
  42.1 0.2 fusion.51
  42.4 0.8 select_reduce_fusion.1
  43.3 0.6 pad_maximum_fusion.3
  43.9 2.8 %collective-permute-start = (bf16[8,4224]{1,0:T(8,128)(2,1)S(1)}, bf16[8,4224]{1,0:T(8,128)(2,1)S(1)}, u32[]{:S(2)}, u32[]{:S(2)}) collective-permute-start(bf16[8,4224]{1,0:T(8,128)(2,1)S(1)} %get-tuple-element.11), channel_id=1, source_target_pairs={{0,8},{1,9},{2,10},{3,11},{4,12},{5,13},{6,14},{7,15},{8,0},{9,1},... | collective-permute-start | bytes 202760 | tf_op jit(solution)/shard_map/ppermute | solution.py:20
  46.8 3.9 %collective-permute-done = bf16[8,4224]{1,0:T(8,128)(2,1)S(1)} collective-permute-done((bf16[8,4224]{1,0:T(8,128)(2,1)S(1)}, bf16[8,4224]{1,0:T(8,128)(2,1)S(1)}, u32[]{:S(2)}, u32[]{:S(2)}) %collective-permute-start) | collective-permute-done | bytes 67616 | tf_op jit(solution)/shard_map/ppermute | solution.py:20
  50.7 0.7 collective-permute-start.1
  51.4 0.6 constant_dynamic-update-slice_fusion.3
  52.0 3.8 %collective-permute-done.1 = bf16[16,4224]{1,0:T(8,128)(2,1)S(1)} collective-permute-done((bf16[16,4224]{1,0:T(8,128)(2,1)S(1)}, bf16[16,4224]{1,0:T(8,128)(2,1)S(1)}, u32[]{:S(2)}, u32[]{:S(2)}) %collective-permute-start.1) | collective-permute-done | bytes 135200 | tf_op jit(solution)/shard_map/ppermute | solution.py:20
  55.8 1.8 %collective-permute-start.2 = (bf16[32,4224]{1,0:T(8,128)(2,1)S(1)}, bf16[32,4224]{1,0:T(8,128)(2,1)S(1)}, u32[]{:S(2)}, u32[]{:S(2)}) collective-permute-start(bf16[32,4224]{1,0:T(8,128)(2,1)S(1)} %pad_maximum_fusion.1), channel_id=1, source_target_pairs={{0,2},{1,3},{2,0},{3,1},{4,6},{5,7},{6,4},{7,5},{8,10},{9,11},{10,... | collective-permute-start | bytes 811016 | tf_op jit(solution)/shard_map/ppermute | solution.py:20
  57.6 0.7 constant_dynamic-update-slice_fusion.2
  58.3 4.0 %collective-permute-done.2 = bf16[32,4224]{1,0:T(8,128)(2,1)S(1)} collective-permute-done((bf16[32,4224]{1,0:T(8,128)(2,1)S(1)}, bf16[32,4224]{1,0:T(8,128)(2,1)S(1)}, u32[]{:S(2)}, u32[]{:S(2)}) %collective-permute-start.2) | collective-permute-done | bytes 270368 | tf_op jit(solution)/shard_map/ppermute | solution.py:20
  62.4 0.7 constant_dynamic-update-slice_fusion.1
  63.2 1.2 %collective-permute-done.3 = bf16[64,4224]{1,0:T(8,128)(2,1)S(1)} collective-permute-done((bf16[64,4224]{1,0:T(8,128)(2,1)S(1)}, bf16[64,4224]{1,0:T(8,128)(2,1)S(1)}, u32[]{:S(2)}, u32[]{:S(2)}) %collective-permute-start.3) | collective-permute-done | bytes 540704 | tf_op jit(solution)/shard_map/ppermute | solution.py:20
  64.4 0.8 constant_dynamic-update-slice_fusion
  65.2 0.9 select_reduce_fusion
  66.1 1.9 %fusion.1 = f32[128,384]{1,0:T(8,128)S(1)} fusion(bf16[1,4096,384]{2,1,0:T(8,128)(2,1)S(1)} %copy-done.2, bf16[128,4224]{1,0:T(8,128)(2,1)} %constant_dynamic-update-slice_fusion), kind=kOutput, calls=%fused_computation.5 | convolution fusion | flops 402653184 | bytes 4390912 | tf_op jit(solution)/shard_map/dot_general | solution.py:80
  68.0 5.0 %convolution_multiply_fusion = f32[128,4096]{1,0:T(8,128)} fusion(bf16[1,384,4096]{2,1,0:T(8,128)(2,1)S(1)} %copy-done, f32[128]{0:T(128)S(1)} %select_reduce_fusion, f32[128,384]{1,0:T(8,128)S(1)} %fusion.1, bf16[1,4096,384]{2,1,0:T(8,128)(2,1)} %param.26, bf16[128,4224]{1,0:T(8,128)(2,1)} %constant_dynamic-update-slice_fusion), kind=kOutput, calls=%fused_computation.3 | convolution fusion | flops 806125568 | bytes 9634304 | tf_op jit(solution)/shard_map/dot_general | solution.py:82
  73.0 1.3 %slice.146 = bf16[64,4096]{1,0:T(8,128)(2,1)S(1)} slice(f32[128,4096]{1,0:T(8,128)} %convolution_multiply_fusion), slice={[64:128], [0:4096]} | slice | bytes 1048576 | tf_op jit(solution)/shard_map/slice | solution.py:85
  74.3 0.2 collective-permute-start.4
  74.5 1.8 %collective-permute-done.4 = bf16[64,4096]{1,0:T(8,128)(2,1)S(1)} collective-permute-done((bf16[64,4096]{1,0:T(8,128)(2,1)S(1)}, bf16[64,4096]{1,0:T(8,128)(2,1)S(1)}, u32[]{:S(2)}, u32[]{:S(2)}) %collective-permute-start.4) | collective-permute-done | bytes 524320 | tf_op jit(solution)/shard_map/ppermute | solution.py:20
  76.3 1.3 %slice_add_fusion = f32[64,4096]{1,0:T(8,128)S(1)} fusion(f32[128,4096]{1,0:T(8,128)} %convolution_multiply_fusion, bf16[64,4096]{1,0:T(8,128)(2,1)S(1)} %collective-permute-done.4), kind=kLoop, calls=%fused_computation.20 | loop fusion | flops 524288 | bytes 2621440 | tf_op jit(solution)/shard_map/add | solution.py:86
  77.6 1.8 %collective-permute-start.5 = (bf16[32,4096]{1,0:T(8,128)(2,1)S(1)}, bf16[32,4096]{1,0:T(8,128)(2,1)S(1)}, u32[]{:S(2)}, u32[]{:S(2)}) collective-permute-start(bf16[32,4096]{1,0:T(8,128)(2,1)S(1)} %slice.147), channel_id=1, source_target_pairs={{0,2},{1,3},{2,0},{3,1},{4,6},{5,7},{6,4},{7,5},{8,10},{9,11},{10,... | collective-permute-start | bytes 786440 | tf_op jit(solution)/shard_map/ppermute | solution.py:20
  79.4 6.6 %collective-permute-done.5 = bf16[32,4096]{1,0:T(8,128)(2,1)S(1)} collective-permute-done((bf16[32,4096]{1,0:T(8,128)(2,1)S(1)}, bf16[32,4096]{1,0:T(8,128)(2,1)S(1)}, u32[]{:S(2)}, u32[]{:S(2)}) %collective-permute-start.5) | collective-permute-done | bytes 262176 | tf_op jit(solution)/shard_map/ppermute | solution.py:20
  86.1 2.2 %collective-permute-start.6 = (bf16[16,4096]{1,0:T(8,128)(2,1)S(1)}, bf16[16,4096]{1,0:T(8,128)(2,1)S(1)}, u32[]{:S(2)}, u32[]{:S(2)}) collective-permute-start(bf16[16,4096]{1,0:T(8,128)(2,1)S(1)} %slice.148), channel_id=1, source_target_pairs={{0,4},{1,5},{2,6},{3,7},{4,0},{5,1},{6,2},{7,3},{8,12},{9,13},{10,... | collective-permute-start | bytes 393224 | tf_op jit(solution)/shard_map/ppermute | solution.py:20
  88.3 2.9 %collective-permute-done.6 = bf16[16,4096]{1,0:T(8,128)(2,1)S(1)} collective-permute-done((bf16[16,4096]{1,0:T(8,128)(2,1)S(1)}, bf16[16,4096]{1,0:T(8,128)(2,1)S(1)}, u32[]{:S(2)}, u32[]{:S(2)}) %collective-permute-start.6) | collective-permute-done | bytes 131104 | tf_op jit(solution)/shard_map/ppermute | solution.py:20
  91.3 4.0 %collective-permute-start.7 = (bf16[8,4096]{1,0:T(8,128)(2,1)S(1)}, bf16[8,4096]{1,0:T(8,128)(2,1)S(1)}, u32[]{:S(2)}, u32[]{:S(2)}) collective-permute-start(bf16[8,4096]{1,0:T(8,128)(2,1)S(1)} %slice.149), channel_id=1, source_target_pairs={{0,8},{1,9},{2,10},{3,11},{4,12},{5,13},{6,14},{7,15},{8,0},{9,1},... | collective-permute-start | bytes 196616 | tf_op jit(solution)/shard_map/ppermute | solution.py:20
  95.3 2.2 %collective-permute-done.7 = bf16[8,4096]{1,0:T(8,128)(2,1)S(1)} collective-permute-done((bf16[8,4096]{1,0:T(8,128)(2,1)S(1)}, bf16[8,4096]{1,0:T(8,128)(2,1)S(1)}, u32[]{:S(2)}, u32[]{:S(2)}) %collective-permute-start.7) | collective-permute-done | bytes 65568 | tf_op jit(solution)/shard_map/ppermute | solution.py:20
  97.6 0.7 fusion.21
  (69 shorter events, 1.2 us)
Async XLA Ops:
  0.0 68.0 %copy-start = (bf16[1,384,4096]{2,1,0:T(8,128)(2,1)S(1)}, bf16[1,384,4096]{2,1,0:T(8,128)(2,1)}, u32[]{:S(2)}) copy-start(bf16[1,384,4096]{2,1,0:T(8,128)(2,1)} %param.28) | copy-start | bytes 9437188
  7.2 25.2 %all-to-all-start = ((bf16[2,16,2,16,256]{4,3,0,2,1:T(8,128)(2,1)}), bf16[2,16,2,16,256]{4,3,0,2,1:T(8,128)(2,1)}, u32[]{:S(2)}, u32[]{:S(2)}) async-start(bf16[2,16,2,16,256]{4,3,0,2,1:T(8,128)(2,1)} %copy.48), calls=%async_computation | async-start | bytes 1048576 | tf_op jit(solution)/shard_map/all_to_all | solution.py:132
  23.0 2.2 %copy-start.7 = (bf16[8,2,256]{2,1,0:T(2,128)(2,1)S(1)}, bf16[8,2,256]{2,1,0:T(2,128)(2,1)}, u32[]{:S(2)}) copy-start(bf16[8,2,256]{2,1,0:T(2,128)(2,1)} %param.17) | copy-start | bytes 24580
  23.0 2.3 %copy-start.13 = (s32[8]{0:T(128)S(1)}, s32[8]{0:T(128)}, u32[]{:S(2)}) copy-start(s32[8]{0:T(128)} %param.20) | copy-start | bytes 100
  23.0 2.4 %copy-start.11 = (bf16[8,4096]{1,0:T(8,128)(2,1)S(1)}, bf16[8,4096]{1,0:T(8,128)(2,1)}, u32[]{:S(2)}) copy-start(bf16[8,4096]{1,0:T(8,128)(2,1)} %param.16) | copy-start | bytes 196612
  25.5 2.1 %copy-start.3 = (bf16[8,256,2,128]{3,2,1,0:T(2,128)(2,1)S(1)}, bf16[8,256,2,128]{3,2,1,0:T(2,128)(2,1)}, u32[]{:S(2)}) copy-start(bf16[8,256,2,128]{3,2,1,0:T(2,128)(2,1)} %reshape_reshape_squeeze.15) | copy-start | bytes 3145732
  27.5 1.2 %copy-start.1 = (s32[16]{0:T(128)S(1)}, s32[16]{0:T(128)}, u32[]{:S(2)}) copy-start(s32[16]{0:T(128)} %param.23) | copy-start | bytes 196
  27.9 6.3 %copy-start.4 = (bf16[8,2,16,128]{3,2,1,0:T(8,128)(2,1)}, bf16[8,2,16,128]{3,2,1,0:T(8,128)(2,1)S(1)}, u32[]{:S(2)}) copy-start(bf16[8,2,16,128]{3,2,1,0:T(8,128)(2,1)S(1)} %fusion.7) | copy-start | bytes 196612
  28.7 5.4 %copy-start.10 = (bf16[1,2,32,128]{3,2,1,0:T(8,128)(2,1)}, bf16[1,2,32,128]{3,2,1,0:T(8,128)(2,1)S(1)}, u32[]{:S(2)}) copy-start(bf16[1,2,32,128]{3,2,1,0:T(8,128)(2,1)S(1)} %copy.66) | copy-start | bytes 49156
  34.9 6.4 %slice-start = ((bf16[8,2,16,128]{3,2,1,0:T(8,128)(2,1)}), bf16[2,2,16,128]{3,2,1,0:T(8,128)(2,1)S(1)}, s32[]{:S(2)}) async-start(bf16[8,2,16,128]{3,2,1,0:T(8,128)(2,1)} %copy-done.4), calls=%async_computation.1 | async-start | bytes 32768 | tf_op jit(solution)/shard_map/slice | solution.py:159
  34.9 6.5 %copy-start.5 = (bf16[8,4096]{1,0:T(8,128)(2,1)S(1)}, bf16[8,4096]{1,0:T(8,128)(2,1)}, u32[]{:S(2)}) copy-start(bf16[8,4096]{1,0:T(8,128)(2,1)} %param.15) | copy-start | bytes 196612
  36.7 4.6 %copy-start.12 = (pred[2]{0:T(512)(128)(4,1)S(1)}, pred[2]{0:T(512)(128)(4,1)}, u32[]{:S(2)}) copy-start(pred[2]{0:T(512)(128)(4,1)} %iota_compare_fusion.6) | copy-start | bytes 10
  36.7 4.9 %copy-start.8 = (f32[4096]{0:T(1024)S(1)}, f32[4096]{0:T(1024)}, u32[]{:S(2)}) copy-start(f32[4096]{0:T(1024)} %param.24) | copy-start | bytes 49156
  36.7 5.0 %copy-start.6 = (bf16[4096,8]{0,1:T(8,128)(2,1)S(1)}, bf16[4096,8]{0,1:T(8,128)(2,1)}, u32[]{:S(2)}) copy-start(bf16[4096,8]{0,1:T(8,128)(2,1)} %param.25) | copy-start | bytes 196612
  36.7 5.2 %copy-start.9 = (s32[8,8]{1,0:T(8,128)S(1)}, s32[8,8]{1,0:T(8,128)}, u32[]{:S(2)}) copy-start(s32[8,8]{1,0:T(8,128)} %param.29) | copy-start | bytes 772
  43.9 6.7 %collective-permute-start = (bf16[8,4224]{1,0:T(8,128)(2,1)S(1)}, bf16[8,4224]{1,0:T(8,128)(2,1)S(1)}, u32[]{:S(2)}, u32[]{:S(2)}) collective-permute-start(bf16[8,4224]{1,0:T(8,128)(2,1)S(1)} %get-tuple-element.11), channel_id=1, source_target_pairs={{0,8},{1,9},{2,10},{3,11},{4,12},{5,13},{6,14},{7,15},{8,0},{9,1},... | collective-permute-start | bytes 202760 | tf_op jit(solution)/shard_map/ppermute | solution.py:20
  50.7 5.1 %collective-permute-start.1 = (bf16[16,4224]{1,0:T(8,128)(2,1)S(1)}, bf16[16,4224]{1,0:T(8,128)(2,1)S(1)}, u32[]{:S(2)}, u32[]{:S(2)}) collective-permute-start(bf16[16,4224]{1,0:T(8,128)(2,1)S(1)} %pad_maximum_fusion.2), channel_id=1, source_target_pairs={{0,4},{1,5},{2,6},{3,7},{4,0},{5,1},{6,2},{7,3},{8,12},{9,13},{10,... | collective-permute-start | bytes 405512 | tf_op jit(solution)/shard_map/ppermute | solution.py:20
  55.8 10.3 %copy-start.2 = (bf16[1,4096,384]{2,1,0:T(8,128)(2,1)S(1)}, bf16[1,4096,384]{2,1,0:T(8,128)(2,1)}, u32[]{:S(2)}) copy-start(bf16[1,4096,384]{2,1,0:T(8,128)(2,1)} %param.27) | copy-start | bytes 9437188
  55.8 6.5 %collective-permute-start.2 = (bf16[32,4224]{1,0:T(8,128)(2,1)S(1)}, bf16[32,4224]{1,0:T(8,128)(2,1)S(1)}, u32[]{:S(2)}, u32[]{:S(2)}) collective-permute-start(bf16[32,4224]{1,0:T(8,128)(2,1)S(1)} %pad_maximum_fusion.1), channel_id=1, source_target_pairs={{0,2},{1,3},{2,0},{3,1},{4,6},{5,7},{6,4},{7,5},{8,10},{9,11},{10,... | collective-permute-start | bytes 811016 | tf_op jit(solution)/shard_map/ppermute | solution.py:20
  62.4 2.0 %collective-permute-start.3 = (bf16[64,4224]{1,0:T(8,128)(2,1)S(1)}, bf16[64,4224]{1,0:T(8,128)(2,1)S(1)}, u32[]{:S(2)}, u32[]{:S(2)}) collective-permute-start(bf16[64,4224]{1,0:T(8,128)(2,1)S(1)} %pad_maximum_fusion), channel_id=1, source_target_pairs={{0,1},{1,0},{2,3},{3,2},{4,5},{5,4},{6,7},{7,6},{8,9},{9,8},{10,11... | collective-permute-start | bytes 1622024 | tf_op jit(solution)/shard_map/ppermute | solution.py:20
  74.3 2.0 %collective-permute-start.4 = (bf16[64,4096]{1,0:T(8,128)(2,1)S(1)}, bf16[64,4096]{1,0:T(8,128)(2,1)S(1)}, u32[]{:S(2)}, u32[]{:S(2)}) collective-permute-start(bf16[64,4096]{1,0:T(8,128)(2,1)S(1)} %slice.146), channel_id=1, source_target_pairs={{0,1},{1,0},{2,3},{3,2},{4,5},{5,4},{6,7},{7,6},{8,9},{9,8},{10,11... | collective-permute-start | bytes 1572872 | tf_op jit(solution)/shard_map/ppermute | solution.py:20
  77.6 8.4 %collective-permute-start.5 = (bf16[32,4096]{1,0:T(8,128)(2,1)S(1)}, bf16[32,4096]{1,0:T(8,128)(2,1)S(1)}, u32[]{:S(2)}, u32[]{:S(2)}) collective-permute-start(bf16[32,4096]{1,0:T(8,128)(2,1)S(1)} %slice.147), channel_id=1, source_target_pairs={{0,2},{1,3},{2,0},{3,1},{4,6},{5,7},{6,4},{7,5},{8,10},{9,11},{10,... | collective-permute-start | bytes 786440 | tf_op jit(solution)/shard_map/ppermute | solution.py:20
  86.1 5.1 %collective-permute-start.6 = (bf16[16,4096]{1,0:T(8,128)(2,1)S(1)}, bf16[16,4096]{1,0:T(8,128)(2,1)S(1)}, u32[]{:S(2)}, u32[]{:S(2)}) collective-permute-start(bf16[16,4096]{1,0:T(8,128)(2,1)S(1)} %slice.148), channel_id=1, source_target_pairs={{0,4},{1,5},{2,6},{3,7},{4,0},{5,1},{6,2},{7,3},{8,12},{9,13},{10,... | collective-permute-start | bytes 393224 | tf_op jit(solution)/shard_map/ppermute | solution.py:20
  91.3 6.2 %collective-permute-start.7 = (bf16[8,4096]{1,0:T(8,128)(2,1)S(1)}, bf16[8,4096]{1,0:T(8,128)(2,1)S(1)}, u32[]{:S(2)}, u32[]{:S(2)}) collective-permute-start(bf16[8,4096]{1,0:T(8,128)(2,1)S(1)} %slice.149), channel_id=1, source_target_pairs={{0,8},{1,9},{2,10},{3,11},{4,12},{5,13},{6,14},{7,15},{8,0},{9,1},... | collective-permute-start | bytes 196616 | tf_op jit(solution)/shard_map/ppermute | solution.py:20
where the time goes:
time: 99.1 us; the launch traced here: 98.2 us
  waiting for transfers between devices  26.4 us (27%)
  local copies, waits for them, and re-layouts  23.2 us (23%)
  starting transfers between devices  21 us (21%)
  other arithmetic  14.7 us (15%)
  matrix products  12.4 us (13%)
    ppermute x8, waiting for transfers between devices, partner(): lax.ppermute(x, axis, [(i, i ^ 1 << apart) for i in range(lax.axis_size(a...  26.4 us
    ppermute x8, starting transfers between devices, partner(): lax.ppermute(x, axis, [(i, i ^ 1 << apart) for i in range(lax.axis_size(a...  13.6 us
    all_to_all x1, starting transfers between devices, local(): lax.all_to_all(outgoing, 'expert', split_axis=1, concat_axis=1, tiled=True)  7.46 us
    unnamed x36, local copies, waits for them, and re-layouts  5.18 us
    dot_general x1, matrix products, all_tokens(): jnp.dot(activated, w_down, preferred_element_type=jnp.float32)  4.98 us
    gather x1, local copies, waits for them, and re-layouts, local(): fetched = local_kv[page_table]  3.07 us
    dot_general x2, matrix products, attend(): jnp.einsum('tkgd,tlkd->tkgl', heads_of_queries, heads_of_keys, preferred_...  3.04 us
    another operation x2, local copies, waits for them, and re-layouts, attend(): rows_of_keys.reshape(decode_tokens, -1, KEY_VALUE_HEADS, HEAD_SIZE)  3 us
  transfers between devices with their start and end apart: 9, of which 8 were waited for; matrix products, arithmetic and copies ran while one was open for 20% of the time, Pallas kernels for 0%

commit v1 on v0

--- a/solution.py
+++ b/solution.py
@@ -129,7 +129,15 @@
         MAXP, devices, 2, PAGE_TOKENS, key_value_width
     )
     outgoing = jnp.where(occupied.T[:, :, None, None, None], outgoing, 0)
-    arrived = lax.all_to_all(outgoing, "expert", split_axis=1, concat_axis=1, tiled=True)
+    ways, here = (lax.axis_size("expert"), lax.axis_index("expert"))
+    width = outgoing.shape[1] // ways
+    turned = jnp.roll(outgoing, -here * width, axis=1)
+    got = [lax.slice_in_dim(turned, 0, width, axis=1)]
+    for far in range(1, ways):
+        sent = lax.slice_in_dim(turned, far * width, (far + 1) * width, axis=1)
+        got.append(lax.ppermute(sent, "expert", [(d, (d + far) % ways) for d in range(ways)]))
+    line = jnp.concatenate(got[::-1], axis=1)
+    arrived = jnp.roll(line, (here + 1) * got[0].shape[1], axis=1)
     lengths = jnp.take(prompt_pages, own_picks)
     new_keys = arrived[:, :, 0].reshape(MAXP, devices * PAGE_TOKENS, key_value_width)
     new_values = arrived[:, :, 1].reshape(MAXP, devices * PAGE_TOKENS, key_value_width)

time: 99.1 us -> 124 us (1.25)
  waiting for transfers between devices: 26.4 us -> 40.4 us
  starting transfers between devices: 21 us -> 25.4 us
  local copies, waits for them, and re-layouts: 23.2 us -> 27.5 us
    ppermute x0 -> x15, starting transfers between devices: none -> 21.8 us  [local(): lax.ppermute(sent, 'expert', [(d, (d + far) % ways) for d in range(ways)])]
    ppermute x8, starting transfers between devices: 13.6 us -> 3.64 us  [partner(): lax.ppermute(x, axis, [(i, i ^ 1 << apart) for i in range(lax.axis_size(a...]
    all_to_all x1 -> x0, starting transfers between devices: 7.46 us -> none  [local(): lax.all_to_all(outgoing, 'expert', split_axis=1, concat_axis=1, tiled=True)]
    ppermute x8, waiting for transfers between devices: 26.4 us -> 33.8 us  [partner(): lax.ppermute(x, axis, [(i, i ^ 1 << apart) for i in range(lax.axis_size(a...]
    ppermute x0 -> x15, waiting for transfers between devices: none -> 6.59 us  [local(): lax.ppermute(sent, 'expert', [(d, (d + far) % ways) for d in range(ways)])]
    unnamed x36 -> x51, local copies, waits for them, and re-layouts: 5.18 us -> 9.82 us
    slice x2 -> x1, local copies, waits for them, and re-layouts: 2.77 us -> 0.74 us  [local(): arrived[:, :, 0].reshape(MAXP, devices * PAGE_TOKENS, key_value_width)]
  transfers between devices with their start and end apart: 9 -> 23, of which waited for: 8 -> 12; matrix products, arithmetic and copies ran while one was open for 20% -> 20% of each run, Pallas kernels for 0% -> 0%
where the time goes in v1:
time: 124 us; the launch traced here: 123 us
  waiting for transfers between devices  40.4 us (33%)
  local copies, waits for them, and re-layouts  27.5 us (22%)
  starting transfers between devices  25.4 us (20%)
  other arithmetic  15.3 us (12%)
  matrix products  13.6 us (11%)
    ppermute x8, waiting for transfers between devices, partner(): lax.ppermute(x, axis, [(i, i ^ 1 << apart) for i in range(lax.axis_size(a...  33.8 us
    ppermute x15, starting transfers between devices, local(): lax.ppermute(sent, 'expert', [(d, (d + far) % ways) for d in range(ways)])  21.8 us
    unnamed x51, local copies, waits for them, and re-layouts  9.82 us
    ppermute x15, waiting for transfers between devices, local(): lax.ppermute(sent, 'expert', [(d, (d + far) % ways) for d in range(ways)])  6.59 us
    dot_general x1, matrix products, all_tokens(): jnp.dot(activated, w_down, preferred_element_type=jnp.float32)  4.98 us
    another operation x2, local copies, waits for them, and re-layouts, attend(): rows_of_values.reshape(decode_tokens, -1, KEY_VALUE_HEADS, HEAD_SIZE)  3.88 us
    ppermute x8, starting transfers between devices, partner(): lax.ppermute(x, axis, [(i, i ^ 1 << apart) for i in range(lax.axis_size(a...  3.64 us
    gather x1, local copies, waits for them, and re-layouts, local(): fetched = local_kv[page_table]  3.07 us
  transfers between devices with their start and end apart: 23, of which 12 were waited for; matrix products, arithmetic and copies ran while one was open for 20% of the time, Pallas kernels for 0%

profile of v1, /device:TPU:0, one launch (start us, length us, event | category | flops | bytes accessed | tf_op | source)
XLA Modules:
  0.0 122.6 jit_solution(13526682850600488801)
XLA Ops:
  0.0 1.0 convert_reduce_fusion
  1.0 0.7 iota_compare_fusion.2
  1.9 0.7 compare_select_fusion
  2.8 2.3 %gather_fusion.1 = bf16[32,2,16,256]{3,2,1,0:T(8,128)(2,1)} fusion(bf16[16,2,16,256]{3,2,1,0:T(8,128)(2,1)} %bitcast.87, s32[1024]{0:T(1024)S(1)} %get-tuple-element.44), kind=kCustom, calls=%fused_computation.1 | custom fusion | bytes 1048704 | tf_op jit(solution)/shard_map/jit(_take)/gather | solution.py:128
  5.1 1.2 fusion.17
  6.6 0.8 copy-done.3
  7.4 0.8 fusion.70
  8.2 5.5 %collective-permute-start = (bf16[2,1,2,16,256]{4,3,1,0,2:T(8,128)(2,1)}, bf16[2,1,2,16,256]{4,3,1,0,2:T(8,128)(2,1)}, u32[]{:S(2)}, u32[]{:S(2)}) collective-permute-start(bf16[2,1,2,16,256]{4,3,1,0,2:T(8,128)(2,1)} %get-tuple-element.26), channel_id=1, source_target_pairs={{0,15},{1,0},{2,1},{3,2},{4,3},{5,4},{6,5},{7,6},{8,7},{9,8},{10,9... | collective-permute-start | bytes 98312 | tf_op jit(solution)/shard_map/ppermute | solution.py:138
  13.7 0.6 collective-permute-start.1
  15.7 3.1 %gather_fusion.2 = bf16[128,2,16,256]{3,2,1,0:T(8,128)(2,1)} fusion(bf16[32,2,16,256]{3,2,1,0:T(8,128)(2,1)} %param.20, s32[1024]{0:T(1024)S(1)} %get-tuple-element.43), kind=kCustom, calls=%fused_computation.2 | custom fusion | bytes 4194816 | tf_op jit(solution)/shard_map/gather | solution.py:155
  18.8 3.1 %slice_bitcast_fusion.1 = (bf16[8,16,1,16,256]{4,3,1,0,2:T(8,128)(2,1)}, bf16[8,16,1,16,256]{4,3,1,0,2:T(8,128)(2,1)}) fusion(bf16[8,16,2,16,256]{4,3,2,1,0:T(8,128)(2,1)} %bitcast.85), kind=kLoop, calls=%fused_computation.22 | loop fusion | bytes 4194304
  21.9 2.1 %reshape_reshape_squeeze.15 = bf16[8,256,2,128]{3,2,1,0:T(2,128)(2,1)} reshape(bf16[8,16,1,16,256]{4,3,1,0,2:T(8,128)(2,1)} %get-tuple-element.9) | data formatting | bytes 2097152 | tf_op jit(solution)/shard_map/reshape;reshape;squeeze | solution.py:29
  24.0 2.2 %reshape_reshape_squeeze.14 = bf16[8,256,2,128]{3,2,1,0:T(2,128)(2,1)} reshape(bf16[8,16,1,16,256]{4,3,1,0,2:T(8,128)(2,1)} %get-tuple-element.8) | data formatting | bytes 2097152 | tf_op jit(solution)/shard_map/reshape;reshape;squeeze | solution.py:28
  26.5 1.7 %fusion.71 = (f32[8,2,16]{2,1,0:T(2,128)S(1)}, f32[8,2,16,256]{3,2,1,0:T(8,128)S(1)}) fusion(bf16[8,2,16,128]{3,0,2,1:T(8,128)(2,1)S(1)} %bitcast.103, bf16[8,256,2,128]{3,2,1,0:T(2,128)(2,1)} %reshape_reshape_squeeze.14, pred[8,256]{1,0:T(8,128)(4,1)S(1)} %broadcast_compare_fusion), kind=kOutput, calls=%fused_computation.167 | convolution fusion | flops 16973568 | bytes 1379328 | tf_op jit(solution)/shard_map/tkgd,tlkd->tkgl/dot_general | solution.py:33
  28.5 0.8 fusion.59
  29.3 0.6 gather_fusion
  30.5 0.7 fusion.56
  31.2 1.5 %fusion.7 = bf16[8,2,16,128]{3,2,1,0:T(8,128)(2,1)S(1)} fusion(bf16[8,256,2,128]{3,2,1,0:T(2,128)(2,1)} %reshape_reshape_squeeze.15, f32[8,2,16,256]{3,2,1,0:T(8,128)S(1)} %get-tuple-element.38, f32[8,2,16]{2,1,0:T(2,128)S(1)} %get-tuple-element.30, f32[8,2,16]{2,1,0:T(2,128)S(1)} %multiply_maximum_fusion, pred[8,256]{1,0:T(8,128)(4,1)S(1)} %broadcast_compare_fusion, ...), kind=kOutput, calls=%fused_computation.13 | convolution fusion | flops 17137664 | bytes 1389568 | tf_op jit(solution)/shard_map/tkgl,tlkd->tkgd/dot_general | solution.py:54
  32.8 1.2 iota_compare_fusion.6
  34.0 4.4 %collective-permute-start.5 = (bf16[2,1,2,16,256]{4,3,1,0,2:T(8,128)(2,1)}, bf16[2,1,2,16,256]{4,3,1,0,2:T(8,128)(2,1)S(1)}, u32[]{:S(2)}, u32[]{:S(2)}) collective-permute-start(bf16[2,1,2,16,256]{4,3,1,0,2:T(8,128)(2,1)} %get-tuple-element.21), channel_id=1, source_target_pairs={{0,10},{1,11},{2,12},{3,13},{4,14},{5,15},{6,0},{7,1},{8,2},{9,3},... | collective-permute-start | bytes 98312 | tf_op jit(solution)/shard_map/ppermute | solution.py:138
  38.4 0.8 constant_dynamic-update-slice_fusion.15
  39.2 0.8 constant_dynamic-update-slice_fusion.14
  39.9 1.6 %collective-permute-start.7 = (bf16[2,1,2,16,256]{4,3,1,0,2:T(8,128)(2,1)}, bf16[2,1,2,16,256]{4,3,1,0,2:T(8,128)(2,1)S(1)}, u32[]{:S(2)}, u32[]{:S(2)}) collective-permute-start(bf16[2,1,2,16,256]{4,3,1,0,2:T(8,128)(2,1)} %get-tuple-element.19), channel_id=1, source_target_pairs={{0,8},{1,9},{2,10},{3,11},{4,12},{5,13},{6,14},{7,15},{8,0},{9,1},... | collective-permute-start | bytes 98312 | tf_op jit(solution)/shard_map/ppermute | solution.py:138
  41.5 0.8 constant_dynamic-update-slice_fusion.13
  42.3 1.1 collective-permute-start.8
  43.4 0.8 constant_dynamic-update-slice_fusion.12
  44.2 2.7 %collective-permute-start.9 = (bf16[2,1,2,16,256]{4,3,1,0,2:T(8,128)(2,1)}, bf16[2,1,2,16,256]{4,3,1,0,2:T(8,128)(2,1)S(1)}, u32[]{:S(2)}, u32[]{:S(2)}) collective-permute-start(bf16[2,1,2,16,256]{4,3,1,0,2:T(8,128)(2,1)} %get-tuple-element.17), channel_id=1, source_target_pairs={{0,6},{1,7},{2,8},{3,9},{4,10},{5,11},{6,12},{7,13},{8,14},{9,15},... | collective-permute-start | bytes 98312 | tf_op jit(solution)/shard_map/ppermute | solution.py:138
  46.8 0.8 constant_dynamic-update-slice_fusion.11
  48.0 2.1 %collective-permute-start.11 = (bf16[2,1,2,16,256]{4,3,1,0,2:T(8,128)(2,1)}, bf16[2,1,2,16,256]{4,3,1,0,2:T(8,128)(2,1)S(1)}, u32[]{:S(2)}, u32[]{:S(2)}) collective-permute-start(bf16[2,1,2,16,256]{4,3,1,0,2:T(8,128)(2,1)} %get-tuple-element.15), channel_id=1, source_target_pairs={{0,4},{1,5},{2,6},{3,7},{4,8},{5,9},{6,10},{7,11},{8,12},{9,13},{1... | collective-permute-start | bytes 98312 | tf_op jit(solution)/shard_map/ppermute | solution.py:138
  50.1 2.0 %collective-permute-start.12 = (bf16[2,1,2,16,256]{4,3,1,0,2:T(8,128)(2,1)}, bf16[2,1,2,16,256]{4,3,1,0,2:T(8,128)(2,1)S(1)}, u32[]{:S(2)}, u32[]{:S(2)}) collective-permute-start(bf16[2,1,2,16,256]{4,3,1,0,2:T(8,128)(2,1)} %get-tuple-element.14), channel_id=1, source_target_pairs={{0,3},{1,4},{2,5},{3,6},{4,7},{5,8},{6,9},{7,10},{8,11},{9,12},{10... | collective-permute-start | bytes 98312 | tf_op jit(solution)/shard_map/ppermute | solution.py:138
  53.3 0.8 collective-permute-done.11
  54.1 2.2 %collective-permute-done.12 = bf16[2,1,2,16,256]{4,3,1,0,2:T(8,128)(2,1)S(1)} collective-permute-done((bf16[2,1,2,16,256]{4,3,1,0,2:T(8,128)(2,1)}, bf16[2,1,2,16,256]{4,3,1,0,2:T(8,128)(2,1)S(1)}, u32[]{:S(2)}, u32[]{:S(2)}) %collective-permute-start.12) | collective-permute-done | bytes 32800 | tf_op jit(solution)/shard_map/ppermute | solution.py:138
  56.3 3.0 %collective-permute-done.13 = bf16[2,1,2,16,256]{4,3,1,0,2:T(8,128)(2,1)S(1)} collective-permute-done((bf16[2,1,2,16,256]{4,3,1,0,2:T(8,128)(2,1)}, bf16[2,1,2,16,256]{4,3,1,0,2:T(8,128)(2,1)S(1)}, u32[]{:S(2)}, u32[]{:S(2)}) %collective-permute-start.13) | collective-permute-done | bytes 32800 | tf_op jit(solution)/shard_map/ppermute | solution.py:138
  59.3 0.8 constant_dynamic-update-slice_fusion
  60.3 0.7 fusion.69
  61.1 1.7 %reshape_reshape_squeeze.13 = bf16[2,256,2,128]{3,2,1,0:T(2,128)(2,1)} reshape(bf16[2,16,1,16,256]{4,3,1,0,2:T(8,128)(2,1)} %get-tuple-element.11) | data formatting | bytes 524288 | tf_op jit(solution)/shard_map/reshape;reshape;squeeze | solution.py:29
  62.8 0.8 reshape_reshape_squeeze.12
  63.6 1.3 %fusion.72 = (f32[2,2,16]{2,1,0:T(2,128)S(1)}, f32[2,2,16,256]{3,2,1,0:T(8,128)S(1)}) fusion(bf16[2,2,16,128]{3,2,1,0:T(8,128)(2,1)} %bitcast.95, bf16[2,256,2,128]{3,2,1,0:T(2,128)(2,1)} %reshape_reshape_squeeze.12, pred[2,256]{1,0:T(4,128)(4,1)} %broadcast_compare_fusion.1), kind=kOutput, calls=%fused_computation.168 | convolution fusion | flops 4243392 | bytes 344832 | tf_op jit(solution)/shard_map/tkgd,tlkd->tkgl/dot_general | solution.py:33
  64.9 0.7 multiply_maximum_fusion.1
  65.5 0.8 fusion.41
  66.3 0.7 fusion.61
  67.0 1.2 fusion.10
  69.3 0.8 select_reduce_fusion.1
  70.2 0.6 pad_maximum_fusion.3
  70.8 1.3 %collective-permute-start.15 = (bf16[8,4224]{1,0:T(8,128)(2,1)S(1)}, bf16[8,4224]{1,0:T(8,128)(2,1)S(1)}, u32[]{:S(2)}, u32[]{:S(2)}) collective-permute-start(bf16[8,4224]{1,0:T(8,128)(2,1)S(1)} %get-tuple-element.27), channel_id=1, source_target_pairs={{0,8},{1,9},{2,10},{3,11},{4,12},{5,13},{6,14},{7,15},{8,0},{9,1},... | collective-permute-start | bytes 202760 | tf_op jit(solution)/shard_map/ppermute | solution.py:20
  72.2 3.8 %collective-permute-done.15 = bf16[8,4224]{1,0:T(8,128)(2,1)S(1)} collective-permute-done((bf16[8,4224]{1,0:T(8,128)(2,1)S(1)}, bf16[8,4224]{1,0:T(8,128)(2,1)S(1)}, u32[]{:S(2)}, u32[]{:S(2)}) %collective-permute-start.15) | collective-permute-done | bytes 67616 | tf_op jit(solution)/shard_map/ppermute | solution.py:20
  76.1 0.6 constant_dynamic-update-slice_fusion.19
  76.7 4.4 %collective-permute-done.16 = bf16[16,4224]{1,0:T(8,128)(2,1)S(1)} collective-permute-done((bf16[16,4224]{1,0:T(8,128)(2,1)S(1)}, bf16[16,4224]{1,0:T(8,128)(2,1)S(1)}, u32[]{:S(2)}, u32[]{:S(2)}) %collective-permute-start.16) | collective-permute-done | bytes 135200 | tf_op jit(solution)/shard_map/ppermute | solution.py:20
  81.2 0.7 constant_dynamic-update-slice_fusion.18
  81.9 5.8 %collective-permute-done.17 = bf16[32,4224]{1,0:T(8,128)(2,1)S(1)} collective-permute-done((bf16[32,4224]{1,0:T(8,128)(2,1)S(1)}, bf16[32,4224]{1,0:T(8,128)(2,1)S(1)}, u32[]{:S(2)}, u32[]{:S(2)}) %collective-permute-start.17) | collective-permute-done | bytes 270368 | tf_op jit(solution)/shard_map/ppermute | solution.py:20
  87.8 0.7 constant_dynamic-update-slice_fusion.17
  88.5 1.2 collective-permute-done.18
  89.7 0.8 constant_dynamic-update-slice_fusion.16
  90.5 0.9 select_reduce_fusion
  91.4 1.9 %fusion.1 = f32[128,384]{1,0:T(8,128)S(1)} fusion(bf16[1,4096,384]{2,1,0:T(8,128)(2,1)S(1)} %copy-done.2, bf16[128,4224]{1,0:T(8,128)(2,1)} %constant_dynamic-update-slice_fusion.16), kind=kOutput, calls=%fused_computation.5 | convolution fusion | flops 402653184 | bytes 4390912 | tf_op jit(solution)/shard_map/dot_general | solution.py:80
  93.4 5.0 %convolution_multiply_fusion = f32[128,4096]{1,0:T(8,128)} fusion(bf16[1,384,4096]{2,1,0:T(8,128)(2,1)S(1)} %copy-done, f32[128]{0:T(128)S(1)} %select_reduce_fusion, f32[128,384]{1,0:T(8,128)S(1)} %fusion.1, bf16[1,4096,384]{2,1,0:T(8,128)(2,1)} %param.28, bf16[128,4224]{1,0:T(8,128)(2,1)} %constant_dynamic-update-slice_fusion.16), kind=kOutput, calls=%fused_computation.3 | convolution fusion | flops 806125568 | bytes 9634304 | tf_op jit(solution)/shard_map/dot_general | solution.py:82
  98.3 1.3 %slice.227 = bf16[64,4096]{1,0:T(8,128)(2,1)S(1)} slice(f32[128,4096]{1,0:T(8,128)} %convolution_multiply_fusion), slice={[64:128], [0:4096]} | slice | bytes 1048576 | tf_op jit(solution)/shard_map/slice | solution.py:85
  99.8 1.8 %collective-permute-done.19 = bf16[64,4096]{1,0:T(8,128)(2,1)S(1)} collective-permute-done((bf16[64,4096]{1,0:T(8,128)(2,1)S(1)}, bf16[64,4096]{1,0:T(8,128)(2,1)S(1)}, u32[]{:S(2)}, u32[]{:S(2)}) %collective-permute-start.19) | collective-permute-done | bytes 524320 | tf_op jit(solution)/shard_map/ppermute | solution.py:20
  101.6 1.3 %slice_add_fusion = f32[64,4096]{1,0:T(8,128)S(1)} fusion(f32[128,4096]{1,0:T(8,128)} %convolution_multiply_fusion, bf16[64,4096]{1,0:T(8,128)(2,1)S(1)} %collective-permute-done.19), kind=kLoop, calls=%fused_computation.20 | loop fusion | flops 524288 | bytes 2621440 | tf_op jit(solution)/shard_map/add | solution.py:86
  103.0 8.3 %collective-permute-done.20 = bf16[32,4096]{1,0:T(8,128)(2,1)S(1)} collective-permute-done((bf16[32,4096]{1,0:T(8,128)(2,1)S(1)}, bf16[32,4096]{1,0:T(8,128)(2,1)S(1)}, u32[]{:S(2)}, u32[]{:S(2)}) %collective-permute-start.20) | collective-permute-done | bytes 262176 | tf_op jit(solution)/shard_map/ppermute | solution.py:20
  111.5 5.0 %collective-permute-done.21 = bf16[16,4096]{1,0:T(8,128)(2,1)S(1)} collective-permute-done((bf16[16,4096]{1,0:T(8,128)(2,1)S(1)}, bf16[16,4096]{1,0:T(8,128)(2,1)S(1)}, u32[]{:S(2)}, u32[]{:S(2)}) %collective-permute-start.21) | collective-permute-done | bytes 131104 | tf_op jit(solution)/shard_map/ppermute | solution.py:20
  116.5 1.8 %collective-permute-start.22 = (bf16[8,4096]{1,0:T(8,128)(2,1)S(1)}, bf16[8,4096]{1,0:T(8,128)(2,1)S(1)}, u32[]{:S(2)}, u32[]{:S(2)}) collective-permute-start(bf16[8,4096]{1,0:T(8,128)(2,1)S(1)} %slice.230), channel_id=1, source_target_pairs={{0,8},{1,9},{2,10},{3,11},{4,12},{5,13},{6,14},{7,15},{8,0},{9,1},... | collective-permute-start | bytes 196616 | tf_op jit(solution)/shard_map/ppermute | solution.py:20
  118.3 3.6 %collective-permute-done.22 = bf16[8,4096]{1,0:T(8,128)(2,1)S(1)} collective-permute-done((bf16[8,4096]{1,0:T(8,128)(2,1)S(1)}, bf16[8,4096]{1,0:T(8,128)(2,1)S(1)}, u32[]{:S(2)}, u32[]{:S(2)}) %collective-permute-start.22) | collective-permute-done | bytes 65568 | tf_op jit(solution)/shard_map/ppermute | solution.py:20
  121.9 0.7 fusion.24
  (113 shorter events, 7.1 us)
Async XLA Ops:
  0.0 93.4 %copy-start = (bf16[1,384,4096]{2,1,0:T(8,128)(2,1)S(1)}, bf16[1,384,4096]{2,1,0:T(8,128)(2,1)}, u32[]{:S(2)}) copy-start(bf16[1,384,4096]{2,1,0:T(8,128)(2,1)} %param.30) | copy-start | bytes 9437188
  6.3 8.8 %copy-start.7 = (bf16[8,2,256]{2,1,0:T(2,128)(2,1)S(1)}, bf16[8,2,256]{2,1,0:T(2,128)(2,1)}, u32[]{:S(2)}) copy-start(bf16[8,2,256]{2,1,0:T(2,128)(2,1)} %param.19) | copy-start | bytes 24580
  6.6 0.8 copy-start.3
  8.2 25.8 %collective-permute-start = (bf16[2,1,2,16,256]{4,3,1,0,2:T(8,128)(2,1)}, bf16[2,1,2,16,256]{4,3,1,0,2:T(8,128)(2,1)}, u32[]{:S(2)}, u32[]{:S(2)}) collective-permute-start(bf16[2,1,2,16,256]{4,3,1,0,2:T(8,128)(2,1)} %get-tuple-element.26), channel_id=1, source_target_pairs={{0,15},{1,0},{2,1},{3,2},{4,3},{5,4},{6,5},{7,6},{8,7},{9,8},{10,9... | collective-permute-start | bytes 98312 | tf_op jit(solution)/shard_map/ppermute | solution.py:138
  13.7 25.5 %collective-permute-start.1 = (bf16[2,1,2,16,256]{4,3,1,0,2:T(8,128)(2,1)}, bf16[2,1,2,16,256]{4,3,1,0,2:T(8,128)(2,1)}, u32[]{:S(2)}, u32[]{:S(2)}) collective-permute-start(bf16[2,1,2,16,256]{4,3,1,0,2:T(8,128)(2,1)} %get-tuple-element.25), channel_id=1, source_target_pairs={{0,14},{1,15},{2,0},{3,1},{4,2},{5,3},{6,4},{7,5},{8,6},{9,7},{10,... | collective-permute-start | bytes 98312 | tf_op jit(solution)/shard_map/ppermute | solution.py:138
  14.3 25.6 %collective-permute-start.2 = (bf16[2,1,2,16,256]{4,3,1,0,2:T(8,128)(2,1)}, bf16[2,1,2,16,256]{4,3,1,0,2:T(8,128)(2,1)}, u32[]{:S(2)}, u32[]{:S(2)}) collective-permute-start(bf16[2,1,2,16,256]{4,3,1,0,2:T(8,128)(2,1)} %get-tuple-element.24), channel_id=1, source_target_pairs={{0,13},{1,14},{2,15},{3,0},{4,1},{5,2},{6,3},{7,4},{8,5},{9,6},{10... | collective-permute-start | bytes 98312 | tf_op jit(solution)/shard_map/ppermute | solution.py:138
  14.5 27.7 %collective-permute-start.3 = (bf16[2,1,2,16,256]{4,3,1,0,2:T(8,128)(2,1)}, bf16[2,1,2,16,256]{4,3,1,0,2:T(8,128)(2,1)}, u32[]{:S(2)}, u32[]{:S(2)}) collective-permute-start(bf16[2,1,2,16,256]{4,3,1,0,2:T(8,128)(2,1)} %get-tuple-element.23), channel_id=1, source_target_pairs={{0,12},{1,13},{2,14},{3,15},{4,0},{5,1},{6,2},{7,3},{8,4},{9,5},{1... | collective-permute-start | bytes 98312 | tf_op jit(solution)/shard_map/ppermute | solution.py:138
  15.0 29.2 %collective-permute-start.4 = (bf16[2,1,2,16,256]{4,3,1,0,2:T(8,128)(2,1)}, bf16[2,1,2,16,256]{4,3,1,0,2:T(8,128)(2,1)}, u32[]{:S(2)}, u32[]{:S(2)}) collective-permute-start(bf16[2,1,2,16,256]{4,3,1,0,2:T(8,128)(2,1)} %get-tuple-element.22), channel_id=1, source_target_pairs={{0,11},{1,12},{2,13},{3,14},{4,15},{5,0},{6,1},{7,2},{8,3},{9,4},{... | collective-permute-start | bytes 98312 | tf_op jit(solution)/shard_map/ppermute | solution.py:138
  24.0 2.2 %copy-start.11 = (bf16[8,4096]{1,0:T(8,128)(2,1)S(1)}, bf16[8,4096]{1,0:T(8,128)(2,1)}, u32[]{:S(2)}) copy-start(bf16[8,4096]{1,0:T(8,128)(2,1)} %param.18) | copy-start | bytes 196612
  24.0 2.3 %copy-start.13 = (s32[8]{0:T(128)S(1)}, s32[8]{0:T(128)}, u32[]{:S(2)}) copy-start(s32[8]{0:T(128)} %param.22) | copy-start | bytes 100
  26.5 2.8 %copy-start.1 = (s32[16]{0:T(128)S(1)}, s32[16]{0:T(128)}, u32[]{:S(2)}) copy-start(s32[16]{0:T(128)} %param.25) | copy-start | bytes 196
  29.2 3.5 %copy-start.10 = (bf16[1,2,32,128]{3,2,1,0:T(8,128)(2,1)}, bf16[1,2,32,128]{3,2,1,0:T(8,128)(2,1)S(1)}, u32[]{:S(2)}) copy-start(bf16[1,2,32,128]{3,2,1,0:T(8,128)(2,1)S(1)} %copy.42) | copy-start | bytes 49156
  32.8 27.5 %copy-start.4 = (bf16[8,2,16,128]{3,2,1,0:T(8,128)(2,1)}, bf16[8,2,16,128]{3,2,1,0:T(8,128)(2,1)S(1)}, u32[]{:S(2)}) copy-start(bf16[8,2,16,128]{3,2,1,0:T(8,128)(2,1)S(1)} %fusion.7) | copy-start | bytes 196612
  34.0 13.6 %collective-permute-start.5 = (bf16[2,1,2,16,256]{4,3,1,0,2:T(8,128)(2,1)}, bf16[2,1,2,16,256]{4,3,1,0,2:T(8,128)(2,1)S(1)}, u32[]{:S(2)}, u32[]{:S(2)}) collective-permute-start(bf16[2,1,2,16,256]{4,3,1,0,2:T(8,128)(2,1)} %get-tuple-element.21), channel_id=1, source_target_pairs={{0,10},{1,11},{2,12},{3,13},{4,14},{5,15},{6,0},{7,1},{8,2},{9,3},... | collective-permute-start | bytes 98312 | tf_op jit(solution)/shard_map/ppermute | solution.py:138
  39.2 8.9 %collective-permute-start.6 = (bf16[2,1,2,16,256]{4,3,1,0,2:T(8,128)(2,1)}, bf16[2,1,2,16,256]{4,3,1,0,2:T(8,128)(2,1)S(1)}, u32[]{:S(2)}, u32[]{:S(2)}) collective-permute-start(bf16[2,1,2,16,256]{4,3,1,0,2:T(8,128)(2,1)} %get-tuple-element.20), channel_id=1, source_target_pairs={{0,9},{1,10},{2,11},{3,12},{4,13},{5,14},{6,15},{7,0},{8,1},{9,2},... | collective-permute-start | bytes 98312 | tf_op jit(solution)/shard_map/ppermute | solution.py:138
  39.9 10.2 %collective-permute-start.7 = (bf16[2,1,2,16,256]{4,3,1,0,2:T(8,128)(2,1)}, bf16[2,1,2,16,256]{4,3,1,0,2:T(8,128)(2,1)S(1)}, u32[]{:S(2)}, u32[]{:S(2)}) collective-permute-start(bf16[2,1,2,16,256]{4,3,1,0,2:T(8,128)(2,1)} %get-tuple-element.19), channel_id=1, source_target_pairs={{0,8},{1,9},{2,10},{3,11},{4,12},{5,13},{6,14},{7,15},{8,0},{9,1},... | collective-permute-start | bytes 98312 | tf_op jit(solution)/shard_map/ppermute | solution.py:138
  42.3 9.9 %collective-permute-start.8 = (bf16[2,1,2,16,256]{4,3,1,0,2:T(8,128)(2,1)}, bf16[2,1,2,16,256]{4,3,1,0,2:T(8,128)(2,1)S(1)}, u32[]{:S(2)}, u32[]{:S(2)}) collective-permute-start(bf16[2,1,2,16,256]{4,3,1,0,2:T(8,128)(2,1)} %get-tuple-element.18), channel_id=1, source_target_pairs={{0,7},{1,8},{2,9},{3,10},{4,11},{5,12},{6,13},{7,14},{8,15},{9,0},... | collective-permute-start | bytes 98312 | tf_op jit(solution)/shard_map/ppermute | solution.py:138
  44.2 8.6 %collective-permute-start.9 = (bf16[2,1,2,16,256]{4,3,1,0,2:T(8,128)(2,1)}, bf16[2,1,2,16,256]{4,3,1,0,2:T(8,128)(2,1)S(1)}, u32[]{:S(2)}, u32[]{:S(2)}) collective-permute-start(bf16[2,1,2,16,256]{4,3,1,0,2:T(8,128)(2,1)} %get-tuple-element.17), channel_id=1, source_target_pairs={{0,6},{1,7},{2,8},{3,9},{4,10},{5,11},{6,12},{7,13},{8,14},{9,15},... | collective-permute-start | bytes 98312 | tf_op jit(solution)/shard_map/ppermute | solution.py:138
  47.6 5.7 %collective-permute-start.10 = (bf16[2,1,2,16,256]{4,3,1,0,2:T(8,128)(2,1)}, bf16[2,1,2,16,256]{4,3,1,0,2:T(8,128)(2,1)S(1)}, u32[]{:S(2)}, u32[]{:S(2)}) collective-permute-start(bf16[2,1,2,16,256]{4,3,1,0,2:T(8,128)(2,1)} %get-tuple-element.16), channel_id=1, source_target_pairs={{0,5},{1,6},{2,7},{3,8},{4,9},{5,10},{6,11},{7,12},{8,13},{9,14},{... | collective-permute-start | bytes 98312 | tf_op jit(solution)/shard_map/ppermute | solution.py:138
  48.0 6.1 %collective-permute-start.11 = (bf16[2,1,2,16,256]{4,3,1,0,2:T(8,128)(2,1)}, bf16[2,1,2,16,256]{4,3,1,0,2:T(8,128)(2,1)S(1)}, u32[]{:S(2)}, u32[]{:S(2)}) collective-permute-start(bf16[2,1,2,16,256]{4,3,1,0,2:T(8,128)(2,1)} %get-tuple-element.15), channel_id=1, source_target_pairs={{0,4},{1,5},{2,6},{3,7},{4,8},{5,9},{6,10},{7,11},{8,12},{9,13},{1... | collective-permute-start | bytes 98312 | tf_op jit(solution)/shard_map/ppermute | solution.py:138
  50.1 6.2 %collective-permute-start.12 = (bf16[2,1,2,16,256]{4,3,1,0,2:T(8,128)(2,1)}, bf16[2,1,2,16,256]{4,3,1,0,2:T(8,128)(2,1)S(1)}, u32[]{:S(2)}, u32[]{:S(2)}) collective-permute-start(bf16[2,1,2,16,256]{4,3,1,0,2:T(8,128)(2,1)} %get-tuple-element.14), channel_id=1, source_target_pairs={{0,3},{1,4},{2,5},{3,6},{4,7},{5,8},{6,9},{7,10},{8,11},{9,12},{10... | collective-permute-start | bytes 98312 | tf_op jit(solution)/shard_map/ppermute | solution.py:138
  52.2 7.2 %collective-permute-start.13 = (bf16[2,1,2,16,256]{4,3,1,0,2:T(8,128)(2,1)}, bf16[2,1,2,16,256]{4,3,1,0,2:T(8,128)(2,1)S(1)}, u32[]{:S(2)}, u32[]{:S(2)}) collective-permute-start(bf16[2,1,2,16,256]{4,3,1,0,2:T(8,128)(2,1)} %get-tuple-element.13), channel_id=1, source_target_pairs={{0,2},{1,3},{2,4},{3,5},{4,6},{5,7},{6,8},{7,9},{8,10},{9,11},{10,... | collective-permute-start | bytes 98312 | tf_op jit(solution)/shard_map/ppermute | solution.py:138
  52.7 6.6 %collective-permute-start.14 = (bf16[2,1,2,16,256]{4,3,1,0,2:T(8,128)(2,1)}, bf16[2,1,2,16,256]{4,3,1,0,2:T(8,128)(2,1)S(1)}, u32[]{:S(2)}, u32[]{:S(2)}) collective-permute-start(bf16[2,1,2,16,256]{4,3,1,0,2:T(8,128)(2,1)} %get-tuple-element.12), channel_id=1, source_target_pairs={{0,1},{1,2},{2,3},{3,4},{4,5},{5,6},{6,7},{7,8},{8,9},{9,10},{10,1... | collective-permute-start | bytes 98312 | tf_op jit(solution)/shard_map/ppermute | solution.py:138
  61.1 7.1 %slice-start = ((bf16[8,2,16,128]{3,2,1,0:T(8,128)(2,1)}), bf16[2,2,16,128]{3,2,1,0:T(8,128)(2,1)S(1)}, s32[]{:S(2)}) async-start(bf16[8,2,16,128]{3,2,1,0:T(8,128)(2,1)} %copy-done.4), calls=%async_computation | async-start | bytes 32768 | tf_op jit(solution)/shard_map/slice | solution.py:167
  61.1 7.2 %copy-start.5 = (bf16[8,4096]{1,0:T(8,128)(2,1)S(1)}, bf16[8,4096]{1,0:T(8,128)(2,1)}, u32[]{:S(2)}) copy-start(bf16[8,4096]{1,0:T(8,128)(2,1)} %param.17) | copy-start | bytes 196612
  63.6 4.6 %copy-start.12 = (pred[2]{0:T(512)(128)(4,1)S(1)}, pred[2]{0:T(512)(128)(4,1)}, u32[]{:S(2)}) copy-start(pred[2]{0:T(512)(128)(4,1)} %iota_compare_fusion.6) | copy-start | bytes 10
  63.6 4.9 %copy-start.8 = (f32[4096]{0:T(1024)S(1)}, f32[4096]{0:T(1024)}, u32[]{:S(2)}) copy-start(f32[4096]{0:T(1024)} %param.26) | copy-start | bytes 49156
  63.6 5.0 %copy-start.6 = (bf16[4096,8]{0,1:T(8,128)(2,1)S(1)}, bf16[4096,8]{0,1:T(8,128)(2,1)}, u32[]{:S(2)}) copy-start(bf16[4096,8]{0,1:T(8,128)(2,1)} %param.27) | copy-start | bytes 196612
  63.6 5.1 %copy-start.9 = (s32[8,8]{1,0:T(8,128)S(1)}, s32[8,8]{1,0:T(8,128)}, u32[]{:S(2)}) copy-start(s32[8,8]{1,0:T(8,128)} %param.31) | copy-start | bytes 772
  70.8 5.2 %collective-permute-start.15 = (bf16[8,4224]{1,0:T(8,128)(2,1)S(1)}, bf16[8,4224]{1,0:T(8,128)(2,1)S(1)}, u32[]{:S(2)}, u32[]{:S(2)}) collective-permute-start(bf16[8,4224]{1,0:T(8,128)(2,1)S(1)} %get-tuple-element.27), channel_id=1, source_target_pairs={{0,8},{1,9},{2,10},{3,11},{4,12},{5,13},{6,14},{7,15},{8,0},{9,1},... | collective-permute-start | bytes 202760 | tf_op jit(solution)/shard_map/ppermute | solution.py:20
  76.0 5.1 %collective-permute-start.16 = (bf16[16,4224]{1,0:T(8,128)(2,1)S(1)}, bf16[16,4224]{1,0:T(8,128)(2,1)S(1)}, u32[]{:S(2)}, u32[]{:S(2)}) collective-permute-start(bf16[16,4224]{1,0:T(8,128)(2,1)S(1)} %pad_maximum_fusion.2), channel_id=1, source_target_pairs={{0,4},{1,5},{2,6},{3,7},{4,0},{5,1},{6,2},{7,3},{8,12},{9,13},{10,... | collective-permute-start | bytes 405512 | tf_op jit(solution)/shard_map/ppermute | solution.py:20
  81.1 10.3 %copy-start.2 = (bf16[1,4096,384]{2,1,0:T(8,128)(2,1)S(1)}, bf16[1,4096,384]{2,1,0:T(8,128)(2,1)}, u32[]{:S(2)}) copy-start(bf16[1,4096,384]{2,1,0:T(8,128)(2,1)} %param.29) | copy-start | bytes 9437188
  81.1 6.5 %collective-permute-start.17 = (bf16[32,4224]{1,0:T(8,128)(2,1)S(1)}, bf16[32,4224]{1,0:T(8,128)(2,1)S(1)}, u32[]{:S(2)}, u32[]{:S(2)}) collective-permute-start(bf16[32,4224]{1,0:T(8,128)(2,1)S(1)} %pad_maximum_fusion.1), channel_id=1, source_target_pairs={{0,2},{1,3},{2,0},{3,1},{4,6},{5,7},{6,4},{7,5},{8,10},{9,11},{10,... | collective-permute-start | bytes 811016 | tf_op jit(solution)/shard_map/ppermute | solution.py:20
  87.7 2.0 %collective-permute-start.18 = (bf16[64,4224]{1,0:T(8,128)(2,1)S(1)}, bf16[64,4224]{1,0:T(8,128)(2,1)S(1)}, u32[]{:S(2)}, u32[]{:S(2)}) collective-permute-start(bf16[64,4224]{1,0:T(8,128)(2,1)S(1)} %pad_maximum_fusion), channel_id=1, source_target_pairs={{0,1},{1,0},{2,3},{3,2},{4,5},{5,4},{6,7},{7,6},{8,9},{9,8},{10,11... | collective-permute-start | bytes 1622024 | tf_op jit(solution)/shard_map/ppermute | solution.py:20
  99.6 2.0 %collective-permute-start.19 = (bf16[64,4096]{1,0:T(8,128)(2,1)S(1)}, bf16[64,4096]{1,0:T(8,128)(2,1)S(1)}, u32[]{:S(2)}, u32[]{:S(2)}) collective-permute-start(bf16[64,4096]{1,0:T(8,128)(2,1)S(1)} %slice.227), channel_id=1, source_target_pairs={{0,1},{1,0},{2,3},{3,2},{4,5},{5,4},{6,7},{7,6},{8,9},{9,8},{10,11... | collective-permute-start | bytes 1572872 | tf_op jit(solution)/shard_map/ppermute | solution.py:20
  103.0 8.4 %collective-permute-start.20 = (bf16[32,4096]{1,0:T(8,128)(2,1)S(1)}, bf16[32,4096]{1,0:T(8,128)(2,1)S(1)}, u32[]{:S(2)}, u32[]{:S(2)}) collective-permute-start(bf16[32,4096]{1,0:T(8,128)(2,1)S(1)} %slice.228), channel_id=1, source_target_pairs={{0,2},{1,3},{2,0},{3,1},{4,6},{5,7},{6,4},{7,5},{8,10},{9,11},{10,... | collective-permute-start | bytes 786440 | tf_op jit(solution)/shard_map/ppermute | solution.py:20
  111.5 5.0 %collective-permute-start.21 = (bf16[16,4096]{1,0:T(8,128)(2,1)S(1)}, bf16[16,4096]{1,0:T(8,128)(2,1)S(1)}, u32[]{:S(2)}, u32[]{:S(2)}) collective-permute-start(bf16[16,4096]{1,0:T(8,128)(2,1)S(1)} %slice.229), channel_id=1, source_target_pairs={{0,4},{1,5},{2,6},{3,7},{4,0},{5,1},{6,2},{7,3},{8,12},{9,13},{10,... | collective-permute-start | bytes 393224 | tf_op jit(solution)/shard_map/ppermute | solution.py:20
  116.5 5.4 %collective-permute-start.22 = (bf16[8,4096]{1,0:T(8,128)(2,1)S(1)}, bf16[8,4096]{1,0:T(8,128)(2,1)S(1)}, u32[]{:S(2)}, u32[]{:S(2)}) collective-permute-start(bf16[8,4096]{1,0:T(8,128)(2,1)S(1)} %slice.230), channel_id=1, source_target_pairs={{0,8},{1,9},{2,10},{3,11},{4,12},{5,13},{6,14},{7,15},{8,0},{9,1},... | collective-permute-start | bytes 196616 | tf_op jit(solution)/shard_map/ppermute | solution.py:20
